TPU v7x, 256 devices: a whole 4x4x8 slice. The times are simulated.
256 devices in a mesh: req: 16 (over y, x), kv: 8 (over z), blk: 2 (over core).
Axes of the slice: x: 4, y: 4, z: 8, core: 2. Of those that a mesh axis runs over, the one named last changes fastest.
Arguments:
- x_resid: bfloat16 [16, 256, 5120], P('req', ('kv', 'blk')), may hold values from -54 to 54
- q_new: bfloat16 [16, 256, 4096], P('req', None, 'kv'), may hold values from -36 to 36
- k_new: bfloat16 [16, 256, 1024], P('req', None, 'kv'), may hold values from -6 to 12
- v_new: bfloat16 [16, 256, 1024], P('req', None, 'kv'), may hold values from -24 to 24
- k_cache: bfloat16 [16, 8, 64, 128, 128], P('req', 'kv', 'blk'), may hold values from -6 to 12
- v_cache: bfloat16 [16, 8, 64, 128, 128], P('req', 'kv', 'blk'), may hold values from -24 to 24
- cache_len: int32 [16], P('req'), may hold values from 1 to 7936, as said below
- page_table: int32 [16, 64], P('req'), may hold values from 0 to 63, as said below
- wo: bfloat16 [4096, 5120], P(('kv', 'blk')), may hold values from -0.09375 to 0.09375
- norm_gain: bfloat16 [5120], replicated, may hold values from 0.099609375 to 1.8984375
- w_gate: bfloat16 [5120, 7168], P('req', ('kv', 'blk')), may hold values from -0.078125 to 0.078125
- w_up: bfloat16 [5120, 7168], P('req', ('kv', 'blk')), may hold values from -0.078125 to 0.078125
- w_down: bfloat16 [7168, 5120], P(('kv', 'blk'), 'req'), may hold values from -0.0625 to 0.0625
Outputs:
- layer_out: bfloat16 [16, 256, 5120], P('req', ('kv', 'blk'))
- k_cache_out: bfloat16 [16, 8, 64, 128, 128], P('req', 'kv', 'blk')
- v_cache_out: bfloat16 [16, 8, 64, 128, 128], P('req', 'kv', 'blk')
Inputs may be any that keep to these rules, and one draw needn't show every extreme that they name: `cache_len`: at least one request has the largest length. `page_table`: each row is a permutation of 0 to 63.
All inputs are finite; a program needn't handle non-finite values.
Results may differ from a plain program's by a relative error of at most 0.0095.
Values may be sent and summed in bfloat16 or wider, within the bound.
A program may use at most 128 MiB of HBM per device.

v0:
```python
import math
import jax
import jax.numpy as jnp
from jax import lax
from jax.sharding import PartitionSpec as P


def combined_all(part, axis, combine):
    gathered = jax.tree.map(lambda a: lax.all_gather(a, axis), part)

    def take(source):
        return jax.tree.map(lambda a: lax.dynamic_index_in_dim(a, source, 0, False), gathered)

    return lax.fori_loop(
        1, lax.axis_size(axis), lambda source, state: combine(state, take(source)), take(0)
    )


def rotate(field, positions):
    half_width = field.shape[-1] // 2
    pair_index = jnp.arange(half_width, dtype=jnp.float32)
    frequency = jnp.power(1000000.0, -2.0 * pair_index / field.shape[-1])
    angles = positions.astype(jnp.float32)[:, None] * frequency[None, :]
    cosine = jnp.cos(angles)
    sine_part = jnp.sin(angles)
    lower_half = field[..., :half_width]
    upper_half = field[..., half_width:]
    return jnp.concatenate(
        [
            lower_half * cosine - upper_half * sine_part,
            upper_half * cosine + lower_half * sine_part,
        ],
        axis=-1,
    )


def merge_parts(first_part, second_part):
    max_first, total_first, out_first = first_part
    max_second, total_second, out_second = second_part
    overall = jnp.maximum(max_first, max_second)
    factor_first = jnp.exp(max_first - overall)
    factor_second = jnp.exp(max_second - overall)
    return (
        overall,
        factor_first * total_first + factor_second * total_second,
        factor_first[..., None] * out_first + factor_second[..., None] * out_second,
    )


def fetch_down(w_down):
    return lax.all_gather(w_down, "req", axis=1, tiled=True)


def rms_rows(rows, norm_gain):
    return (
        rows
        * lax.rsqrt(jnp.mean(rows * rows, axis=-1, keepdims=True) + 1e-05)
        * norm_gain.astype(jnp.float32)
    ).astype(jnp.bfloat16)


def on_device(
    x_resid,
    q_new,
    k_new,
    v_new,
    k_cache,
    v_cache,
    cache_len,
    page_table,
    wo,
    norm_gain,
    w_gate,
    w_up,
    w_down,
):
    blk_count = lax.axis_size("blk")
    blk_id = lax.axis_index("blk")
    new_tokens = q_new.shape[1]
    head_dim = k_new.shape[2]
    group_size = q_new.shape[2] // head_dim
    slot_count = k_cache.shape[2]
    page_size = k_cache.shape[3]
    page_total = page_table.shape[1]
    length = cache_len[0]
    positions = length + jnp.arange(new_tokens, dtype=jnp.int32)
    query_heads = rotate(
        q_new[0].reshape(new_tokens, group_size, head_dim).astype(jnp.float32).transpose(1, 0, 2),
        positions,
    ).astype(jnp.bfloat16)
    fresh_keys = rotate(k_new[0].astype(jnp.float32), positions).astype(jnp.bfloat16)
    page_ids = jnp.arange(page_total, dtype=jnp.int32)
    physical = blk_id * slot_count + jnp.arange(slot_count, dtype=jnp.int32)
    logical = jnp.sum(
        jnp.where(page_table[0][None, :] == physical[:, None], page_ids[None, :], 0), axis=1
    )
    slot_position = (
        logical[:, None] * page_size + jnp.arange(page_size, dtype=jnp.int32)[None, :]
    ).reshape(slot_count * page_size)
    new_index = slot_position - length
    is_new = (new_index >= 0) & (new_index < new_tokens)
    chosen = jnp.clip(new_index, 0, new_tokens - 1)
    key_rows = jnp.where(
        is_new[:, None], fresh_keys[chosen], k_cache[0, 0].reshape(slot_count * page_size, head_dim)
    )
    value_rows = jnp.where(
        is_new[:, None], v_new[0][chosen], v_cache[0, 0].reshape(slot_count * page_size, head_dim)
    )
    scores = jnp.einsum(
        "qd,sd->qs",
        query_heads.reshape(group_size * new_tokens, head_dim),
        key_rows,
        preferred_element_type=jnp.float32,
    ) * (1.0 / math.sqrt(head_dim))
    scores = scores.reshape(group_size, new_tokens, slot_count * page_size)
    allowed = slot_position[None, None, :] <= positions[None, :, None]
    masked = jnp.where(allowed, scores, -1e30)
    block_max = jnp.max(masked, axis=-1)
    weights = jnp.where(allowed, jnp.exp(masked - block_max[..., None]), 0.0).astype(jnp.bfloat16)
    block_total = jnp.sum(weights.astype(jnp.float32), axis=-1)
    block_out = jnp.einsum("gcs,sd->gcd", weights, value_rows, preferred_element_type=jnp.float32)
    merged = combined_all((block_max, block_total, block_out), "blk", merge_parts)
    attn = (merged[2] / merged[1][..., None]).astype(jnp.bfloat16)
    per_core = group_size // blk_count
    mine = lax.dynamic_slice_in_dim(attn, blk_id * per_core, per_core, 0)
    mine_rows = mine.transpose(1, 0, 2).reshape(new_tokens, per_core * head_dim)
    token_rows = x_resid.shape[1]
    row_start = lax.axis_index(("kv", "blk")) * token_rows
    partial_value = jnp.dot(mine_rows, wo, preferred_element_type=jnp.float32)
    own_part = lax.dynamic_slice_in_dim(partial_value, row_start, token_rows, 0) + x_resid[
        0
    ].astype(jnp.float32)
    contrib = lax.dynamic_update_slice_in_dim(partial_value, own_part, row_start, 0)
    resid = lax.psum(contrib, ("kv", "blk"))
    normed = rms_rows(resid, norm_gain)
    own_resid = lax.dynamic_slice_in_dim(resid, row_start, token_rows, 0)
    gate_val = jnp.dot(
        normed,
        lax.all_gather(w_gate, "req", axis=0, tiled=True),
        preferred_element_type=jnp.float32,
    )
    up_val = jnp.dot(
        normed, lax.all_gather(w_up, "req", axis=0, tiled=True), preferred_element_type=jnp.float32
    )
    hidden = (jax.nn.silu(gate_val) * up_val).astype(jnp.bfloat16)
    down_full = fetch_down(w_down)
    mlp_rows = lax.psum_scatter(
        jnp.dot(hidden, down_full, preferred_element_type=jnp.float32).astype(jnp.bfloat16),
        ("kv", "blk"),
        scatter_dimension=0,
        tiled=True,
    ).astype(jnp.float32)
    layer_out = (own_resid + mlp_rows).astype(jnp.bfloat16)[None]
    return (layer_out, key_rows.reshape(k_cache.shape), value_rows.reshape(v_cache.shape))


def solution(mesh):
    in_specs = (
        P("req", ("kv", "blk"), None),
        P("req", None, "kv"),
        P("req", None, "kv"),
        P("req", None, "kv"),
        P("req", "kv", "blk", None, None),
        P("req", "kv", "blk", None, None),
        P("req"),
        P("req", None),
        P(("kv", "blk"), None),
        P(),
        P("req", ("kv", "blk")),
        P("req", ("kv", "blk")),
        P(("kv", "blk"), "req"),
    )
    out_specs = (
        P("req", ("kv", "blk"), None),
        P("req", "kv", "blk", None, None),
        P("req", "kv", "blk", None, None),
    )
    return jax.shard_map(
        on_device, mesh=mesh, in_specs=in_specs, out_specs=out_specs, check_vma=False
    )
```

profile of v0, /device:TPU:2, one launch (start us, length us, event | category | flops | bytes accessed | tf_op | source)
XLA Modules:
  0.0 365.1 jit_solution(288112992523952814)
XLA Ops:
  8.0 0.0 all-gather.12.cloned.1.call-start
  8.9 0.9 copy.31
  9.9 0.3 multiply_cosine_fusion
  10.2 0.1 copy.32
  10.3 0.8 select_reduce_fusion
  11.2 0.1 fusion.16
  11.3 0.1 compare_and_fusion
  11.4 1.9 reshape.295
  13.3 1.3 copy.30
  14.6 0.1 subtract_convert_fusion
  14.8 15.0 %gather_fusion = bf16[4096,128]{1,0:T(8,128)(2,1)} fusion(bf16[256,128]{1,0:T(8,128)(2,1)S(1)} %copy.32, s32[4096]{0:T(1024)S(1)} %broadcast_clamp_fusion), kind=kCustom, calls=%fused_computation | custom fusion | bytes 2113536 | tf_op jit(solution)/shard_map/gather | solution.py:104
  29.8 15.0 %gather_fusion.1 = bf16[4096,128]{1,0:T(8,128)(2,1)} fusion(bf16[256,128]{1,0:T(8,128)(2,1)S(1)} %bitcast.87, s32[4096]{0:T(1024)S(1)} %broadcast_clamp_fusion), kind=kCustom, calls=%fused_computation.1 | custom fusion | bytes 2113536 | tf_op jit(solution)/shard_map/gather | solution.py:107
  44.8 0.1 fusion.20
  44.9 0.6 broadcast_compare_fusion
  45.6 3.6 bitcast_select_fusion.2
  49.2 3.7 %fusion.1 = (f32[1024]{0:T(1024)S(1)}, f32[1024,4096]{1,0:T(8,128)S(1)}) fusion(pred[256,4096]{1,0:T(8,128)(4,1)S(1)} %broadcast_compare_fusion, bf16[4096,128]{1,0:T(8,128)(2,1)S(1)} %bitcast_select_fusion.2, bf16[1024,64]{0,1:T(8,128)(2,1)S(1)} %bitcast.95, bf16[1024,64]{0,1:T(8,128)(2,1)S(1)} %bitcast.94), kind=kOutput, calls=%fused_computation.6 | convolution fusion | flops 1086848000 | bytes 19140608 | tf_op jit(solution)/shard_map/qd,sd->qs/dot_general | solution.py:109
  52.9 6.7 %convert_reduce_fusion = (f32[1024]{0:T(1024)S(1)}, bf16[1024,4096]{1,0:T(8,128)(2,1)S(1)}) fusion(f32[1024]{0:T(1024)S(1)} %get-tuple-element.46, f32[1024,4096]{1,0:T(8,128)S(1)} %get-tuple-element.47, pred[256,4096]{1,0:T(8,128)(4,1)S(1)} %broadcast_compare_fusion), kind=kLoop, calls=%fused_computation.5 | loop fusion | flops 29359104 | bytes 26222592 | tf_op jit(solution)/shard_map/reduce_sum | solution.py:120
  59.7 1.5 broadcast_select_fusion
  61.2 1.0 copy-done.6
  62.2 3.2 fusion.34
  65.3 0.0 all-gather.12.cloned.1.call-update
  65.4 0.0 all-reduce.2.cloned.1.call-start
  65.4 1.8 all_gather.32
  67.3 2.0 all_gather.28
  69.3 13.5 %all-gather.12.cloned.1.call-done = f32[8,256,128]{2,1,0:T(8,128)} async-done(((f32[4,256,128]{2,1,0:T(8,128)}), f32[8,256,128]{2,1,0:T(8,128)}) %all-gather.12.cloned.1.call-update) | async-done | bytes 1048592 | tf_op jit(solution)/shard_map/all_gather | solution.py:9
  82.8 1.3 fusion.33
  84.1 0.8 copy.37
  85.0 0.1 copy.38
  85.1 1.0 divide_convert_fusion
  86.2 3.2 fusion.35
  89.4 1.7 fusion.8
  91.1 0.0 all-reduce.2.cloned.1.call-update
  91.1 0.0 all-gather.6.cloned.1.call-start
  91.2 0.5 all-gather.6.cloned.1.call-update
  91.7 0.0 all-gather.10.cloned.1.call-start
  91.7 0.5 all-gather.10.cloned.1.call-update
  92.3 0.0 all-gather.8.cloned.1.call-start
  92.3 0.5 all-gather.8.cloned.1.call-update
  92.9 0.0 reduce-scatter.2.cloned.1.call-start
  92.9 126.8 %all-reduce.2.cloned.1.call-done = f32[256,5120]{1,0:T(8,128)} async-done(((f32[256,5120]{1,0:T(8,128)}), f32[256,5120]{1,0:T(8,128)}) %all-reduce.2.cloned.1.call-update) | async-done | bytes 5242896 | tf_op jit(solution)/shard_map/psum | solution.py:134
  219.8 2.9 multiply_reduce_fusion
  222.7 0.0 all-gather.6.cloned.1.call-done
  222.7 6.2 %fusion.29 = f32[256,448]{0,1:T(8,128)S(1)} fusion(bf16[5120,448]{1,0:T(8,128)(2,1)} %all-gather.6.cloned.1.call-done, f32[256,5120]{1,0:T(8,128)} %all-reduce.2.cloned.1.call-done, f32[5120]{0:T(1024)S(1)} %convert_element_type.69, f32[256]{0:T(256)S(1)} %add_rsqrt_fusion), kind=kOutput, calls=%fused_computation.74 | convolution fusion | flops 1178337280 | bytes 10310656 | tf_op jit(solution)/shard_map/dot_general | solution.py:137
  228.9 0.0 all-gather.10.cloned.1.call-done
  228.9 53.8 %all-gather.8.cloned.1.call-done = bf16[5120,448]{1,0:T(8,128)(2,1)} async-done(((bf16[320,448]{1,0:T(8,128)(2,1)}), bf16[5120,448]{1,0:T(8,128)(2,1)}) %all-gather.8.cloned.1.call-update) | async-done | bytes 4587536 | tf_op jit(solution)/shard_map/all_gather | solution.py:143
  282.8 12.4 %convolution_convert_fusion = bf16[256,5120]{1,0:T(8,128)(2,1)} fusion(bf16[448,5120]{0,1:T(8,128)(2,1)} %all-gather.10.cloned.1.call-done, bf16[5120,448]{1,0:T(8,128)(2,1)} %all-gather.8.cloned.1.call-done, f32[256,448]{0,1:T(8,128)S(1)} %fusion.29, f32[256,5120]{1,0:T(8,128)} %all-reduce.2.cloned.1.call-done, f32[5120]{0:T(1024)S(1)} %convert_element_type.69, ...), kind=kOutput, calls=%fused_computation.7 | convolution fusion | flops 2354741248 | bytes 17519616 | tf_op jit(solution)/shard_map/dot_general | solution.py:148
  295.2 60.8 %reduce-scatter.2.cloned.1.call-done = bf16[16,5120]{1,0:T(8,128)(2,1)} async-done(((bf16[256,5120]{1,0:T(8,128)(2,1)}), bf16[16,5120]{1,0:T(8,128)(2,1)}) %reduce-scatter.2.cloned.1.call-update) | async-done | bytes 163856 | tf_op jit(solution)/shard_map/reduce_scatter | solution.py:147
  356.0 1.8 fusion.14
  (38 shorter events, 0.3 us)
Async XLA Ops:
  8.0 78.2 %copy-start = (bf16[256,5120]{1,0:T(8,128)(2,1)S(1)}, bf16[256,5120]{1,0:T(8,128)(2,1)}, u32[]{:S(2)}) copy-start(bf16[256,5120]{1,0:T(8,128)(2,1)} %param.21) | copy-start | bytes 7864324
  8.0 74.8 %all-gather.12.cloned.1.call-start = ((), (), s32[]{:S(2)}) async-start(), calls=%async_computation.6 | async-start | bytes 1572864 | tf_op jit(solution)/shard_map/all_gather | solution.py:9
  14.6 15.2 %copy-start.1 = (bf16[1,256,128]{2,1,0:T(8,128)(2,1)S(1)}, bf16[1,256,128]{2,1,0:T(8,128)(2,1)}, u32[]{:S(2)}) copy-start(bf16[1,256,128]{2,1,0:T(8,128)(2,1)} %param.16) | copy-start | bytes 196612
  52.9 6.8 %copy-start.2 = (bf16[4096,128]{1,0:T(8,128)(2,1)S(1)}, bf16[4096,128]{1,0:T(8,128)(2,1)}, u32[]{:S(2)}) copy-start(bf16[4096,128]{1,0:T(8,128)(2,1)} %gather_fusion) | copy-start | bytes 3145732
  52.9 6.8 %copy-start.3 = (bf16[4096,128]{1,0:T(8,128)(2,1)S(1)}, bf16[4096,128]{1,0:T(8,128)(2,1)}, u32[]{:S(2)}) copy-start(bf16[4096,128]{1,0:T(8,128)(2,1)} %gather_fusion.1) | copy-start | bytes 3145732
  52.9 6.8 %copy-start.4 = (bf16[1,1,32,128,128]{4,3,2,1,0:T(8,128)(2,1)S(1)}, bf16[1,1,32,128,128]{4,3,2,1,0:T(8,128)(2,1)}, u32[]{:S(2)}) copy-start(bf16[1,1,32,128,128]{4,3,2,1,0:T(8,128)(2,1)} %param.17) | copy-start | bytes 3145732
  52.9 6.8 %copy-start.5 = (bf16[1,1,32,128,128]{4,3,2,1,0:T(8,128)(2,1)S(1)}, bf16[1,1,32,128,128]{4,3,2,1,0:T(8,128)(2,1)}, u32[]{:S(2)}) copy-start(bf16[1,1,32,128,128]{4,3,2,1,0:T(8,128)(2,1)} %param.18) | copy-start | bytes 3145732
  61.2 1.0 copy-start.6
  65.4 154.4 %all-reduce.2.cloned.1.call-start = ((), (), s32[]{:S(2)}) async-start(), calls=%async_computation.1 | async-start | bytes 10485760 | tf_op jit(solution)/shard_map/psum | solution.py:134
  85.0 4.4 %copy-start.7 = (bf16[1,16,5120]{2,1,0:T(8,128)(2,1)S(1)}, bf16[1,16,5120]{2,1,0:T(8,128)(2,1)}, u32[]{:S(2)}) copy-start(bf16[1,16,5120]{2,1,0:T(8,128)(2,1)} %param.13) | copy-start | bytes 491524
  89.4 3.6 copy-start.8
  91.1 131.6 %all-gather.6.cloned.1.call-start = ((), (), s32[]{:S(2)}) async-start(), calls=%async_computation.2 | async-start | bytes 5570560 | tf_op jit(solution)/shard_map/all_gather | solution.py:139
  91.7 137.2 %all-gather.10.cloned.1.call-start = ((), (), s32[]{:S(2)}) async-start(), calls=%async_computation.4 | async-start | bytes 5570560 | tf_op jit(solution)/shard_map/all_gather | solution.py:51
  92.3 190.5 %all-gather.8.cloned.1.call-start = ((), (), s32[]{:S(2)}) async-start(), calls=%async_computation.3 | async-start | bytes 5570560 | tf_op jit(solution)/shard_map/all_gather | solution.py:143
  92.9 263.1 %reduce-scatter.2.cloned.1.call-start = ((), (), s32[]{:S(2)}) async-start(), calls=%async_computation.5 | async-start | bytes 2785280 | tf_op jit(solution)/shard_map/reduce_scatter | solution.py:147
Sparse Core Ops, SparseCore 0:
  65.5 17.2 all-gather.11
  91.2 128.4 all-reduce.1
  295.3 60.6 reduce-scatter.1
Sparse Core Ops, SparseCore 1:
  94.0 62.4 all-gather.5
  158.8 60.7 all-gather.9
  221.9 60.8 all-gather.7
where the time goes:
time: 365 us
  waiting for transfers between devices  257 us (70%)
  local copies, waits for them, and re-layouts  37.7 us (10%)
  matrix products  28.6 us (8%)
  other arithmetic  21.5 us (6%)
  between operations  16.6 us (5%)
  blocking collectives  3.81 us (1%)
    psum x1, waiting for transfers between devices, on_device(): resid = lax.psum(contrib, ('kv', 'blk'))  127 us
    reduce_scatter x1, waiting for transfers between devices, on_device(): lax.psum_scatter(jnp.dot(hidden, down_full, preferred_element_type=jnp.fl...  60.8 us
    all_gather x1, waiting for transfers between devices, on_device(): lax.all_gather(w_up, 'req', axis=0, tiled=True)  53.8 us
    gather x1, local copies, waits for them, and re-layouts, on_device(): fresh_keys[chosen]  15 us
    gather x1, local copies, waits for them, and re-layouts, on_device(): v_new[0][chosen]  15 us
    all_gather x1, waiting for transfers between devices, combined_all(): gathered = jax.tree.map(lambda a: lax.all_gather(a, axis), part)  13.5 us
    dot_general x1, matrix products, on_device(): jnp.dot(hidden, down_full, preferred_element_type=jnp.float32)  12.4 us
  transfers between devices with their start and end apart: 6, of which 4 were waited for; matrix products, arithmetic and copies ran while one was open for 2% of the time, Pallas kernels for 0%

commit v1 on v0

--- a/solution.py
+++ b/solution.py
@@ -131,7 +131,7 @@
         0
     ].astype(jnp.float32)
     contrib = lax.dynamic_update_slice_in_dim(partial_value, own_part, row_start, 0)
-    resid = lax.psum(contrib, ("kv", "blk"))
+    resid = jnp.sum(lax.all_gather(contrib, ("kv", "blk")), axis=0)
     normed = rms_rows(resid, norm_gain)
     own_resid = lax.dynamic_slice_in_dim(resid, row_start, token_rows, 0)
     gate_val = jnp.dot(

time: 365 us -> 773 us (2.12)
  waiting for transfers between devices: 257 us -> 638 us
  other arithmetic: 21.5 us -> 49.4 us
    all_gather x0 -> x1, waiting for transfers between devices: none -> 411 us  [on_device(): resid = jnp.sum(lax.all_gather(contrib, ('kv', 'blk')), axis=0)]
    psum x1 -> x0, waiting for transfers between devices: 127 us -> none  [on_device(): resid = lax.psum(contrib, ('kv', 'blk'))]
    all_gather x1, waiting for transfers between devices: 0.03 us -> 63.3 us  [fetch_down(): return lax.all_gather(w_down, 'req', axis=1, tiled=True)]
    all_gather x1, waiting for transfers between devices: 0.03 us -> 30.4 us  [on_device(): lax.all_gather(w_gate, 'req', axis=0, tiled=True)]
    reduce_sum x0 -> x1, other arithmetic: none -> 28.9 us  [on_device(): resid = jnp.sum(lax.all_gather(contrib, ('kv', 'blk')), axis=0)]
  transfers between devices with their start and end apart: 6 -> 6, of which waited for: 4 -> 6; matrix products, arithmetic and copies ran while one was open for 2% -> 5% of each run, Pallas kernels for 0% -> 0%
where the time goes in v1:
time: 773 us
  waiting for transfers between devices  638 us (83%)
  other arithmetic  49.4 us (6%)
  local copies, waits for them, and re-layouts  40 us (5%)
  matrix products  26.4 us (3%)
  between operations  15.2 us (2%)
    all_gather x1, waiting for transfers between devices, on_device(): resid = jnp.sum(lax.all_gather(contrib, ('kv', 'blk')), axis=0)  411 us
    all_gather x1, waiting for transfers between devices, fetch_down(): return lax.all_gather(w_down, 'req', axis=1, tiled=True)  63.3 us
    reduce_scatter x1, waiting for transfers between devices, on_device(): lax.psum_scatter(jnp.dot(hidden, down_full, preferred_element_type=jnp.fl...  60.7 us
    all_gather x1, waiting for transfers between devices, on_device(): lax.all_gather(w_up, 'req', axis=0, tiled=True)  57.1 us
    all_gather x1, waiting for transfers between devices, on_device(): lax.all_gather(w_gate, 'req', axis=0, tiled=True)  30.4 us
    reduce_sum x1, other arithmetic, on_device(): resid = jnp.sum(lax.all_gather(contrib, ('kv', 'blk')), axis=0)  28.9 us
  transfers between devices with their start and end apart: 6, of which 6 were waited for; matrix products, arithmetic and copies ran while one was open for 5% of the time, Pallas kernels for 0%

profile of v1, /device:TPU:2, one launch (start us, length us, event | category | flops | bytes accessed | tf_op | source)
XLA Modules:
  0.0 772.8 jit_solution(13690909916491767472)
XLA Ops:
  7.2 0.0 all-gather.15.cloned.1.call-start
  8.1 0.9 copy.31
  9.0 0.3 multiply_cosine_fusion
  9.4 0.1 copy.32
  9.5 0.8 select_reduce_fusion
  10.3 0.1 fusion.17
  10.5 0.1 compare_and_fusion
  10.5 1.9 reshape.297
  12.4 1.3 copy.30
  13.7 0.1 subtract_convert_fusion
  13.9 15.0 %gather_fusion = bf16[4096,128]{1,0:T(8,128)(2,1)} fusion(bf16[256,128]{1,0:T(8,128)(2,1)S(1)} %copy.32, s32[4096]{0:T(1024)S(1)} %broadcast_clamp_fusion), kind=kCustom, calls=%fused_computation | custom fusion | bytes 2113536 | tf_op jit(solution)/shard_map/gather | solution.py:104
  29.0 15.0 %gather_fusion.1 = bf16[4096,128]{1,0:T(8,128)(2,1)} fusion(bf16[256,128]{1,0:T(8,128)(2,1)S(1)} %bitcast.92, s32[4096]{0:T(1024)S(1)} %broadcast_clamp_fusion), kind=kCustom, calls=%fused_computation.1 | custom fusion | bytes 2113536 | tf_op jit(solution)/shard_map/gather | solution.py:107
  44.0 0.1 fusion.21
  44.1 0.6 broadcast_compare_fusion
  44.7 3.6 bitcast_select_fusion.2
  48.3 3.7 fusion.1
  52.1 6.7 convert_reduce_fusion
  58.9 1.5 broadcast_select_fusion
  60.4 1.0 copy-done.7
  61.3 3.2 fusion.35
  64.5 0.0 all-gather.7.cloned.1.call-start
  64.6 1.8 all_gather.40
  66.4 2.0 all_gather.36
  68.5 13.5 %all-gather.15.cloned.1.call-done = f32[8,256,128]{2,1,0:T(8,128)} async-done(((f32[4,256,128]{2,1,0:T(8,128)}), f32[8,256,128]{2,1,0:T(8,128)}) %all-gather.15.cloned.1.call-update) | async-done | bytes 1048592 | tf_op jit(solution)/shard_map/all_gather | solution.py:9
  82.0 1.3 fusion.34
  83.3 0.8 copy.37
  84.1 0.1 copy.38
  84.3 1.0 divide_convert_fusion
  85.3 0.9 fusion.36
  86.2 2.3 copy.41
  88.5 0.8 fusion.9
  89.3 0.0 all-gather.9.cloned.1.call-start
  89.4 0.7 all-gather.9.cloned.1.call-update
  90.1 0.0 all-gather.11.cloned.1.call-start
  90.1 0.5 all-gather.11.cloned.1.call-update
  90.6 0.0 all-gather.13.cloned.1.call-start
  90.7 0.5 all-gather.13.cloned.1.call-update
  91.2 0.0 reduce-scatter.2.cloned.1.call-start
  91.3 410.9 %all-gather.7.cloned.1.call-done = f32[16,256,5120]{2,1,0:T(8,128)} async-done(((f32[1,256,5120]{2,1,0:T(8,128)}), f32[16,256,5120]{2,1,0:T(8,128)}) %all-gather.7.cloned.1.call-update) | async-done | bytes 83886096 | tf_op jit(solution)/shard_map/all_gather | solution.py:134
  502.2 28.9 %reduce_sum.38 = f32[256,5120]{1,0:T(8,128)} reduce(f32[16,256,5120]{2,1,0:T(8,128)} %all-gather.7.cloned.1.call-done, f32[]{:T(128)} %constant.66.clone.1), dimensions={0}, to_apply=%region_3.4 | reduce | flops 19660800 | bytes 89128960 | tf_op jit(solution)/shard_map/reduce_sum | solution.py:134
  531.1 2.9 multiply_reduce_fusion
  534.0 30.4 %all-gather.9.cloned.1.call-done = bf16[5120,448]{1,0:T(8,128)(2,1)} async-done(((bf16[320,448]{1,0:T(8,128)(2,1)}), bf16[5120,448]{1,0:T(8,128)(2,1)}) %all-gather.9.cloned.1.call-update) | async-done | bytes 4587536 | tf_op jit(solution)/shard_map/all_gather | solution.py:139
  564.4 6.1 fusion.30
  570.6 57.1 %all-gather.11.cloned.1.call-done = bf16[5120,448]{1,0:T(8,128)(2,1)} async-done(((bf16[320,448]{1,0:T(8,128)(2,1)}), bf16[5120,448]{1,0:T(8,128)(2,1)}) %all-gather.11.cloned.1.call-update) | async-done | bytes 4587536 | tf_op jit(solution)/shard_map/all_gather | solution.py:143
  627.7 63.3 %all-gather.13.cloned.1.call-done = bf16[448,5120]{0,1:T(8,128)(2,1)} async-done(((bf16[448,320]{0,1:T(8,128)(2,1)}), bf16[448,5120]{0,1:T(8,128)(2,1)}) %all-gather.13.cloned.1.call-update) | async-done | bytes 4587536 | tf_op jit(solution)/shard_map/all_gather | solution.py:51
  691.0 12.5 %convolution_convert_fusion = bf16[256,5120]{1,0:T(8,128)(2,1)} fusion(bf16[448,5120]{0,1:T(8,128)(2,1)} %all-gather.13.cloned.1.call-done, bf16[5120,448]{1,0:T(8,128)(2,1)} %all-gather.11.cloned.1.call-done, f32[256,448]{0,1:T(8,128)S(1)} %fusion.30, f32[256,5120]{1,0:T(8,128)} %reduce_sum.38, f32[5120]{0:T(1024)S(1)} %convert_element_type.69, ...), kind=kOutput, calls=%fused_computation.7 | convolution fusion | flops 2354741248 | bytes 17519616 | tf_op jit(solution)/shard_map/dot_general | solution.py:148
  703.5 60.7 %reduce-scatter.2.cloned.1.call-done = bf16[16,5120]{1,0:T(8,128)(2,1)} async-done(((bf16[256,5120]{1,0:T(8,128)(2,1)}), bf16[16,5120]{1,0:T(8,128)(2,1)}) %reduce-scatter.2.cloned.1.call-update) | async-done | bytes 163856 | tf_op jit(solution)/shard_map/reduce_scatter | solution.py:147
  764.2 1.8 fusion.15
  (42 shorter events, 0.3 us)
Async XLA Ops:
  7.2 78.1 %copy-start = (bf16[256,5120]{1,0:T(8,128)(2,1)S(1)}, bf16[256,5120]{1,0:T(8,128)(2,1)}, u32[]{:S(2)}) copy-start(bf16[256,5120]{1,0:T(8,128)(2,1)} %param.21) | copy-start | bytes 7864324
  7.2 74.8 %all-gather.15.cloned.1.call-start = ((), (), s32[]{:S(2)}) async-start(), calls=%async_computation.6 | async-start | bytes 1572864 | tf_op jit(solution)/shard_map/all_gather | solution.py:9
  13.7 15.2 %copy-start.2 = (bf16[1,256,128]{2,1,0:T(8,128)(2,1)S(1)}, bf16[1,256,128]{2,1,0:T(8,128)(2,1)}, u32[]{:S(2)}) copy-start(bf16[1,256,128]{2,1,0:T(8,128)(2,1)} %param.16) | copy-start | bytes 196612
  52.1 6.8 copy-start.3
  52.1 6.8 copy-start.4
  52.1 6.8 copy-start.5
  52.1 6.8 copy-start.6
  60.4 1.0 copy-start.7
  64.5 437.7 %all-gather.7.cloned.1.call-start = ((), (), s32[]{:S(2)}) async-start(), calls=%async_computation.1 | async-start | bytes 89128960 | tf_op jit(solution)/shard_map/all_gather | solution.py:134
  86.2 2.4 copy-start.8
  88.5 2.7 copy-start.9
  89.3 475.1 %all-gather.9.cloned.1.call-start = ((), (), s32[]{:S(2)}) async-start(), calls=%async_computation.2 | async-start | bytes 5570560 | tf_op jit(solution)/shard_map/all_gather | solution.py:139
  90.1 537.7 %all-gather.11.cloned.1.call-start = ((), (), s32[]{:S(2)}) async-start(), calls=%async_computation.3 | async-start | bytes 5570560 | tf_op jit(solution)/shard_map/all_gather | solution.py:143
  90.6 600.4 %all-gather.13.cloned.1.call-start = ((), (), s32[]{:S(2)}) async-start(), calls=%async_computation.4 | async-start | bytes 5570560 | tf_op jit(solution)/shard_map/all_gather | solution.py:51
  91.2 673.0 %reduce-scatter.2.cloned.1.call-start = ((), (), s32[]{:S(2)}) async-start(), calls=%async_computation.5 | async-start | bytes 2785280 | tf_op jit(solution)/shard_map/reduce_scatter | solution.py:147
  691.0 74.9 %copy-start.1 = (bf16[256,5120]{1,0:T(8,128)(2,1)S(1)}, bf16[256,5120]{1,0:T(8,128)(2,1)}, u32[]{:S(2)}) copy-start(bf16[256,5120]{1,0:T(8,128)(2,1)} %param.21) | copy-start | bytes 7864324
Sparse Core Ops, SparseCore 0:
  64.6 17.3 all-gather.14
  89.4 412.7 all-gather.6
  504.6 59.7 all-gather.8
  566.7 60.9 all-gather.10
  630.0 60.9 all-gather.12
  703.7 60.4 reduce-scatter.1
